TPU v7x, 32 devices: a whole 2x2x4 slice. The times are simulated.
32 devices in a mesh: row: 4 (over x, core), col: 8 (over z, y).
Axes of the slice: x: 2, y: 2, z: 4, core: 2. Of those that a mesh axis runs over, the one named last changes fastest.
Arguments:
- heat_source: bfloat16 [262144, 128], P(('row', 'col')), may hold values from -6 to 6
- diagonal: float32 [262144], P(('row', 'col')), may hold values from 3 to 8
- active: int32 [262144], P(('row', 'col')), may hold values 0 or 1
- conductance: bfloat16 [2048, 7, 128, 128], P(('row', 'col')), may hold values from -0.1875 to 0.1875
- pattern: int32 [2048, 7], P(('row', 'col')), may hold values from 0 to 127, as said below
- send_list: int32 [32, 4, 16], P(('row', 'col')), may hold values from 0 to 63
- owner_map: int32 [2, 2048], replicated, may hold values from 0 to 63, as said below
- displacement: bfloat16 [64, 32, 128, 128], P('row', 'col'), may hold values from -6 to 6
- bond_live: int32 [6, 64, 32, 128], P(None, 'row', 'col'), may hold values from 0 to 1, as said below
Outputs:
- brick_temperature: bfloat16 [64, 32, 128, 128], P('row', 'col')
- moved: bfloat16 [64, 32, 128, 128], P('row', 'col')
Inputs may be any that keep to these rules, and one draw needn't show every extreme that they name: `pattern`: tile 0 of a block row reads the block itself (its row within the device); tile 1 reads received slot 64 + that row. `owner_map`: every brick slot receives exactly one block. Brick slot s is fed from the device a fixed cyclic distance back along the curve order, the same distance for every brick; one device sends exactly 2 blocks to some bricks and at most that to any. bond_live[d + 3] at a cell equals bond_live[d] at the cell one step back along direction d, and 0 where that cell lies outside the grid; bonds leaving the grid in + directions are 0. `send_list`: local block indices.
All inputs are finite; a program needn't handle non-finite values. No bound on the sum of `active` on one device may be relied on, other than what follows from the above.
Results may differ from a plain program's by a relative error of at most 0.004.
Values may be sent and summed in bfloat16 or wider, within the bound.
A program may use at most 192 MiB of HBM per device.

v0:
```python
import jax
import jax.numpy as jnp
from jax import lax
from jax.sharding import PartitionSpec as P

ITERS = 3


LOWER = 1.0
UPPER = 10.0
ALPHA_T = 0.5
BOND_STIFFNESS = 1.0
STATE_STIFFNESS = 2.0
STEP_SIZE = 0.1
GHOST_STEPS = (1, -1, 2, -2)


def passed_along(value, axis, steps):
    count = lax.axis_size(axis)
    leading, last = (max(0, -steps), min(count, count - steps))
    return lax.ppermute(value, axis, [(source, source + steps) for source in range(leading, last)])


def with_halo(shard, sides, width):
    for axis, dim in sides:
        size, length = (lax.axis_size(axis), shard.shape[dim])
        up = [(i, (i + 1) % size) for i in range(size - 1)]
        down = [(j, i) for i, j in up]
        last = lax.slice_in_dim(shard, length - width, length, axis=dim)
        leading = lax.slice_in_dim(shard, 0, width, axis=dim)
        before = lax.ppermute(last, axis, up)
        after = lax.ppermute(leading, axis, down)
        shard = jnp.concatenate([before, shard, after], axis=dim)
    return shard


def chebyshev_weights(count):
    center = (UPPER + LOWER) / 2.0
    half_width = (UPPER - LOWER) / 2.0
    ratio_value = center / half_width
    previous = 1.0 / ratio_value
    weights = []
    for step_number in range(count):
        current = 1.0 / (2.0 * ratio_value - previous)
        weights.append((current * previous, 2.0 * current / half_width))
        previous = current
    return (1.0 / center, weights)


def along_depth(field, sign):
    size = field.shape[2]
    padded = jnp.pad(field, ((0, 0), (0, 0), (1, 1), (0, 0)))
    return lax.slice_in_dim(padded, 1 + sign, 1 + sign + size, axis=2)


def adjacent_cells(extended, bond_count):
    if bond_count == 0:
        return extended[2:, 1:-1]
    if bond_count == 1:
        return extended[1:-1, 2:]
    if bond_count == 3:
        return extended[:-2, 1:-1]
    if bond_count == 4:
        return extended[1:-1, :-2]
    inner = extended[1:-1, 1:-1]
    return along_depth(inner, 1 if bond_count == 2 else -1)


def local(
    heat_source,
    diagonal,
    active,
    conductance,
    pattern,
    send_list,
    owner_map,
    displacement,
    bond_live,
):
    resident_blocks = conductance.shape[0]
    tile_count = conductance.shape[1]
    block_length = conductance.shape[2]
    scenario_batch = heat_source.shape[1]
    active_f = active.astype(jnp.float32)
    first_scale, weights = chebyshev_weights(ITERS)
    residual = heat_source.astype(jnp.float32)
    pair_unit_vector = residual * first_scale
    computed_heat_map = jnp.zeros_like(residual)
    for old_weight, res_weight in weights:
        masked = (
            (pair_unit_vector * active_f[:, None])
            .astype(jnp.bfloat16)
            .reshape(resident_blocks, block_length, scenario_batch)
        )
        received = []
        for group_num, step_by in enumerate(GHOST_STEPS):
            apply_outgoing = masked[send_list[0, group_num]]
            received.append(passed_along(apply_outgoing, ("row", "col"), step_by))
        apply_extended = jnp.concatenate([masked] + received, 0)
        total = jnp.zeros((resident_blocks, block_length, scenario_batch), jnp.float32)
        for tile_k in range(tile_count):
            chosen = apply_extended[pattern[:, tile_k]]
            total = total + jnp.einsum(
                "bij,bjr->bir", conductance[:, tile_k], chosen, preferred_element_type=jnp.float32
            )
        image = diagonal[:, None] * pair_unit_vector + active_f[:, None] * total.reshape(
            -1, scenario_batch
        )
        computed_heat_map = computed_heat_map + pair_unit_vector
        residual = residual - image
        pair_unit_vector = old_weight * pair_unit_vector + res_weight * residual
    thermal_profile = (
        (computed_heat_map + pair_unit_vector)
        .astype(jnp.bfloat16)
        .reshape(resident_blocks, block_length, scenario_batch)
    )
    devices = lax.axis_size(("row", "col"))
    own_index = lax.axis_index(("row", "col"))
    relay_cap = max(1, resident_blocks // devices)
    dest_all = owner_map[0]
    slot_all = owner_map[1]
    dest_rows = dest_all.reshape(devices, resident_blocks)
    earlier = jnp.tril(jnp.ones((resident_blocks, resident_blocks), jnp.bool_), -1)
    rank_all = jnp.sum(
        ((dest_rows[:, :, None] == dest_rows[:, None, :]) & earlier[None]).astype(jnp.int32), axis=2
    )
    flat_all = (jnp.arange(devices, dtype=jnp.int32)[:, None] * relay_cap + rank_all).reshape(-1)
    start_row = own_index * resident_blocks
    my_dest = lax.dynamic_slice_in_dim(dest_all, start_row, resident_blocks)
    my_rank = lax.dynamic_slice_in_dim(rank_all.reshape(-1), start_row, resident_blocks)
    outgoing = (
        jnp.zeros((devices * relay_cap, block_length, scenario_batch), jnp.bfloat16)
        .at[my_dest * relay_cap + my_rank]
        .set(thermal_profile)
    )
    arrived = lax.all_to_all(outgoing, ("row", "col"), split_axis=0, concat_axis=0, tiled=True)
    mine = dest_all == own_index
    slot_match = (
        slot_all[None, :] == jnp.arange(resident_blocks, dtype=jnp.int32)[:, None]
    ) & mine[None, :]
    source_row = jnp.sum(jnp.where(slot_match, flat_all[None, :], 0), axis=1)
    lattice_nodes = arrived[source_row].reshape(displacement.shape)
    fields = jnp.stack([displacement, lattice_nodes])
    extended = with_halo(fields, (("row", 1), ("col", 2)), 1)
    moving_ext = extended[0].astype(jnp.float32)
    heat_ext = extended[1].astype(jnp.float32)
    moving = moving_ext[1:-1, 1:-1]
    heat = heat_ext[1:-1, 1:-1]
    live = bond_live.astype(jnp.float32)
    bond_stretches = []
    volume_dilatation = jnp.zeros_like(moving)
    for bond_count in range(6):
        stretch = (
            adjacent_cells(moving_ext, bond_count)
            - moving
            - ALPHA_T * 0.5 * (heat + adjacent_cells(heat_ext, bond_count))
        )
        bond_stretches.append(stretch)
        volume_dilatation = volume_dilatation + live[bond_count][..., None] * stretch
    volume_dilatation = volume_dilatation / 6.0
    dilatation_extended = with_halo(
        volume_dilatation.astype(jnp.bfloat16), (("row", 0), ("col", 1)), 1
    ).astype(volume_dilatation.dtype)
    force = jnp.zeros_like(moving)
    for bond_count in range(6):
        series_term = BOND_STIFFNESS * bond_stretches[bond_count] + STATE_STIFFNESS * (
            adjacent_cells(dilatation_extended, bond_count) - volume_dilatation
        )
        force = force + live[bond_count][..., None] * series_term
    moved = (moving + STEP_SIZE * force).astype(jnp.bfloat16)
    return (lattice_nodes, moved)


def solution(mesh):
    return jax.shard_map(
        local,
        mesh=mesh,
        in_specs=(
            P(("row", "col"), None),
            P(("row", "col")),
            P(("row", "col")),
            P(("row", "col"), None, None, None),
            P(("row", "col"), None),
            P(("row", "col"), None, None),
            P(),
            P("row", "col", None, None),
            P(None, "row", "col", None),
        ),
        out_specs=(P("row", "col", None, None), P("row", "col", None, None)),
        check_vma=False,
    )
```

profile of v0, /device:TPU:8, one launch (start us, length us, event | category | flops | bytes accessed | tf_op | source)
XLA Modules:
  0.0 602.2 jit_solution(15410031079041845164)
XLA Ops:
  25.4 6.8 %collective-permute-done = bf16[16,128,128]{2,1,0:T(8,128)(2,1)S(1)} collective-permute-done((bf16[16,128,128]{2,1,0:T(8,128)(2,1)}, bf16[16,128,128]{2,1,0:T(8,128)(2,1)S(1)}, u32[]{:S(2)}, u32[]{:S(2)}) %collective-permute-start) | collective-permute-done | bytes 524320 | tf_op jit(solution)/shard_map/ppermute | solution.py:21
  37.9 12.0 %collective-permute-done.3 = bf16[16,128,128]{2,1,0:T(8,128)(2,1)S(1)} collective-permute-done((bf16[16,128,128]{2,1,0:T(8,128)(2,1)}, bf16[16,128,128]{2,1,0:T(8,128)(2,1)S(1)}, u32[]{:S(2)}, u32[]{:S(2)}) %collective-permute-start.3) | collective-permute-done | bytes 524320 | tf_op jit(solution)/shard_map/ppermute | solution.py:21
  54.0 4.3 gather_fusion.9
  62.6 5.1 fusion.72
  67.7 4.4 fusion.78
  72.0 4.3 gather_fusion.7
  76.4 5.0 fusion.84
  85.7 4.9 fusion.90
  99.2 5.1 fusion.102
  104.2 4.6 fusion.96
  109.7 8.8 %add_add_fusion.2 = f32[64,128,128]{1,2,0:T(8,128)S(1)} fusion(f32[64,128,128]{1,2,0:T(8,128)S(1)} %copy-done.7, f32[64,128,128]{1,2,0:T(8,128)S(1)} %copy-done.8, f32[64,128,128]{1,2,0:T(8,128)} %fusion.84, f32[64,128,128]{1,2,0:T(8,128)} %fusion.90, f32[64,128,128]{1,2,0:T(8,128)} %fusion.102, f32[64,128,128]{1,2,0:T(8,128)} %fusion.96, ...), kind=kOutput, calls=%fused_computation.121 | convolution fusion | flops 274726912 | bytes 33554432 | tf_op jit(solution)/shard_map/bij,bjr->bir/dot_general | solution.py:103
  118.6 4.4 multiply_convert_fusion.1
  127.7 4.8 collective-permute-start.5
  143.7 4.4 collective-permute-done.4
  155.1 12.0 %collective-permute-done.7 = bf16[16,128,128]{2,1,0:T(8,128)(2,1)S(1)} collective-permute-done((bf16[16,128,128]{2,1,0:T(8,128)(2,1)}, bf16[16,128,128]{2,1,0:T(8,128)(2,1)S(1)}, u32[]{:S(2)}, u32[]{:S(2)}) %collective-permute-start.7) | collective-permute-done | bytes 524320 | tf_op jit(solution)/shard_map/ppermute | solution.py:21
  180.9 4.4 gather_fusion.18
  185.3 4.4 gather_fusion.17
  194.1 4.5 gather_fusion.15
  198.6 5.0 fusion.74
  203.6 4.5 fusion.80
  208.1 4.6 fusion.86
  221.1 12.3 %add_add_fusion.1 = f32[64,128,128]{1,2,0:T(8,128)} fusion(f32[64,128,128]{1,2,0:T(8,128)} %fusion.74, f32[64,128,128]{1,2,0:T(8,128)} %fusion.80, f32[64,128,128]{1,2,0:T(8,128)} %fusion.86, f32[64,128,128]{1,2,0:T(8,128)} %fusion.92, f32[64,128,128]{1,2,0:T(8,128)} %fusion.104, f32[64,128,128]{1,2,0:T(8,128)} %fusion.98, ...), kind=kOutput, calls=%fused_computation.120 | convolution fusion | flops 274726912 | bytes 33554432 | tf_op jit(solution)/shard_map/bij,bjr->bir/dot_general | solution.py:103
  233.4 6.8 %multiply_convert_fusion = bf16[8192,128]{1,0:T(8,128)(2,1)S(1)} fusion(f32[64,128,128]{1,2,0:T(8,128)} %add_add_fusion.1, bf16[8192,128]{1,0:T(8,128)(2,1)} %param.9, f32[64,128,128]{1,2,0:T(8,128)} %copy-done.3, f32[8192]{0:T(1024)S(1)} %copy-done.21, f32[8192]{0:T(1024)S(1)} %convert_element_type.54, f32[8192]{0:T(1024)S(1)} %broadcast_multiply_fusion.1), kind=kLoop, calls=%fused_computation.124 | loop fusion | flops 17825792 | bytes 12681216 | tf_op jit(solution)/shard_map/convert_element_type | solution.py:92
  245.1 4.8 collective-permute-start.9
  255.7 4.9 collective-permute-start.11
  266.3 4.8 collective-permute-done.9
  275.0 9.0 %collective-permute-done.11 = bf16[16,128,128]{2,1,0:T(8,128)(2,1)S(1)} collective-permute-done((bf16[16,128,128]{2,1,0:T(8,128)(2,1)}, bf16[16,128,128]{2,1,0:T(8,128)(2,1)S(1)}, u32[]{:S(2)}, u32[]{:S(2)}) %collective-permute-start.11) | collective-permute-done | bytes 524320 | tf_op jit(solution)/shard_map/ppermute | solution.py:21
  297.8 4.4 gather_fusion.29
  302.2 4.3 gather_fusion.28
  306.5 4.4 gather_fusion.27
  310.9 4.5 gather_fusion.26
  315.4 5.1 fusion.106
  320.5 4.6 fusion.100
  325.0 4.5 fusion.94
  337.9 12.3 %add_add_fusion = f32[64,128,128]{1,2,0:T(8,128)} fusion(f32[64,128,128]{1,2,0:T(8,128)} %fusion.76, f32[64,128,128]{1,2,0:T(8,128)} %fusion.82, f32[64,128,128]{1,2,0:T(8,128)} %fusion.88, f32[64,128,128]{1,2,0:T(8,128)} %fusion.94, f32[64,128,128]{1,2,0:T(8,128)} %fusion.106, f32[64,128,128]{1,2,0:T(8,128)} %fusion.100, ...), kind=kOutput, calls=%fused_computation.119 | convolution fusion | flops 274726912 | bytes 33554432 | tf_op jit(solution)/shard_map/bij,bjr->bir/dot_general | solution.py:103
  350.2 7.2 %fusion.26 = bf16[8192,128]{1,0:T(8,128)(2,1)S(1)} fusion(bf16[8192,128]{1,0:T(8,128)(2,1)} %param.9, f32[64,128,128]{1,2,0:T(8,128)} %add_add_fusion, f32[64,128,128]{1,2,0:T(8,128)} %add_add_fusion.1, f32[64,128,128]{1,2,0:T(8,128)} %copy-done.3, f32[8192]{0:T(1024)S(1)} %copy-done.21, f32[8192]{0:T(1024)S(1)} %convert_element_type.54, ...), kind=kLoop, calls=%fused_computation.73 | loop fusion | flops 28311552 | bytes 16875520 | tf_op jit(solution)/shard_map/convert_element_type | solution.py:114
  359.3 8.6 %scatter_fusion = bf16[64,128,128]{2,1,0:T(8,128)(2,1)} fusion(bf16[64,128,128]{2,1,0:T(8,128)(2,1)} %broadcast_in_dim.13, s32[64]{0:T(128)S(1)} %compare_select_fusion.12, bf16[64,128,128]{2,1,0:T(8,128)(2,1)S(1)} %bitcast.225), kind=kCustom, calls=%fused_computation.34 | custom fusion | bytes 6291712 | tf_op jit(solution)/shard_map/scatter | solution.py:134
  367.9 4.9 all-to-all-start
  373.2 46.7 %all-to-all-done = bf16[64,128,128]{2,1,0:T(8,128)(2,1)} async-done(((bf16[64,128,128]{2,1,0:T(8,128)(2,1)}), bf16[64,128,128]{2,1,0:T(8,128)(2,1)}, u32[]{:S(2)}, u32[]{:S(2)}) %all-to-all-start) | async-done | bytes 2097184 | tf_op jit(solution)/shard_map/all_to_all | solution.py:136
  433.0 5.1 collective-permute-start.15
  438.2 42.7 %collective-permute-done.14 = bf16[2,18,1,128,128]{4,3,2,1,0:T(8,128)(2,1)S(1)} collective-permute-done((bf16[2,18,1,128,128]{4,3,2,1,0:T(8,128)(2,1)S(1)}, bf16[2,18,1,128,128]{4,3,2,1,0:T(8,128)(2,1)S(1)}, u32[]{:S(2)}, u32[]{:S(2)}) %collective-permute-start.14) | collective-permute-done | bytes 1179680 | tf_op jit(solution)/shard_map/ppermute | solution.py:31
  480.8 7.1 %collective-permute-done.15 = bf16[2,18,1,128,128]{4,3,2,1,0:T(8,128)(2,1)S(1)} collective-permute-done((bf16[2,18,1,128,128]{4,3,2,1,0:T(8,128)(2,1)S(1)}, bf16[2,18,1,128,128]{4,3,2,1,0:T(8,128)(2,1)S(1)}, u32[]{:S(2)}, u32[]{:S(2)}) %collective-permute-start.15) | collective-permute-done | bytes 1179680 | tf_op jit(solution)/shard_map/ppermute | solution.py:32
  491.7 4.8 fusion.59
  504.0 30.0 %fusion.57 = (bf16[16,4,128,128]{3,2,1,0:T(8,128)(2,1)S(1)}, f32[16,4,128,128]{3,2,1,0:T(8,128)}, f32[16,4,128,128]{3,2,1,0:T(8,128)}, f32[16,4,128,128]{3,2,1,0:T(8,128)}, f32[16,4,128,128]{3,2,1,0:T(8,128)}) fusion(f32[16,4,128]{2,1,0:T(4,128)S(1)} %get-tuple-element.18, f32[16,4,128]{2,1,0:T(4,128)S(1)} %get-tuple-element.19, ...), kind=kLoop, calls=%fused_computation.123 | loop fusion | flops 38797312 | bytes 69402624 | tf_op jit(solution)/shard_map/convert_element_type | solution.py:162
  541.7 5.1 collective-permute-start.19
  546.8 18.8 %collective-permute-done.18 = bf16[18,1,128,128]{3,2,1,0:T(8,128)(2,1)S(1)} collective-permute-done((bf16[18,1,128,128]{3,2,1,0:T(8,128)(2,1)S(1)}, bf16[18,1,128,128]{3,2,1,0:T(8,128)(2,1)S(1)}, u32[]{:S(2)}, u32[]{:S(2)}) %collective-permute-start.18) | collective-permute-done | bytes 589856 | tf_op jit(solution)/shard_map/ppermute | solution.py:31
  565.6 5.7 collective-permute-done.19
  576.2 25.6 %fusion.18 = bf16[16,4,128,128]{3,2,1,0:T(8,128)(2,1)} fusion(f32[16,4,128,128]{3,2,1,0:T(8,128)} %slice.365, f32[16,4,128,128]{3,2,1,0:T(8,128)} %get-tuple-element.6, f32[18,6,128,128]{3,2,1,0:T(8,128)} %copy-done.2, f32[16,4,128,128]{3,2,1,0:T(8,128)} %get-tuple-element.5, f32[16,4,128,128]{3,2,1,0:T(8,128)} %get-tuple-element.4, ...), kind=kLoop, calls=%fused_computation.65 | loop fusion | flops 54525952 | bytes 52625408 | tf_op jit(solution)/shard_map/convert_element_type | solution.py:170
  (187 shorter events, 183.3 us)
Async XLA Ops:
  2.2 21.5 %copy-start.25 = (s32[64,7]{0,1:T(8,128)S(1)}, s32[64,7]{0,1:T(8,128)}, u32[]{:S(2)}) copy-start(s32[64,7]{0,1:T(8,128)} %param.13) | copy-start | bytes 5380
  2.2 21.6 %copy-start.21 = (f32[8192]{0:T(1024)S(1)}, f32[8192]{0:T(1024)}, u32[]{:S(2)}) copy-start(f32[8192]{0:T(1024)} %param.10) | copy-start | bytes 98308
  2.2 21.6 %copy-start.23 = (s32[8192]{0:T(1024)S(1)}, s32[8192]{0:T(1024)}, u32[]{:S(2)}) copy-start(s32[8192]{0:T(1024)} %param.11) | copy-start | bytes 98308
  6.2 26.0 %collective-permute-start = (bf16[16,128,128]{2,1,0:T(8,128)(2,1)}, bf16[16,128,128]{2,1,0:T(8,128)(2,1)S(1)}, u32[]{:S(2)}, u32[]{:S(2)}) collective-permute-start(bf16[16,128,128]{2,1,0:T(8,128)(2,1)} %gather_fusion), channel_id=1, source_target_pairs={{0,1},{1,2},{2,3},{3,4},{4,5},{5,6},{6,7},{7,8},{8,9},{9,10},{10,1... | collective-permute-start | bytes 1572872 | tf_op jit(solution)/shard_map/ppermute | solution.py:21
  11.0 23.2 %collective-permute-start.1 = (bf16[16,128,128]{2,1,0:T(8,128)(2,1)}, bf16[16,128,128]{2,1,0:T(8,128)(2,1)}, u32[]{:S(2)}, u32[]{:S(2)}) collective-permute-start(bf16[16,128,128]{2,1,0:T(8,128)(2,1)} %gather_fusion.1), channel_id=1, source_target_pairs={{1,0},{2,1},{3,2},{4,3},{5,4},{6,5},{7,6},{8,7},{9,8},{10,9},{11,1... | collective-permute-start | bytes 1572872 | tf_op jit(solution)/shard_map/ppermute | solution.py:21
  15.7 20.3 %collective-permute-start.2 = (bf16[16,128,128]{2,1,0:T(8,128)(2,1)}, bf16[16,128,128]{2,1,0:T(8,128)(2,1)}, u32[]{:S(2)}, u32[]{:S(2)}) collective-permute-start(bf16[16,128,128]{2,1,0:T(8,128)(2,1)} %gather_fusion.2), channel_id=1, source_target_pairs={{0,2},{1,3},{2,4},{3,5},{4,6},{5,7},{6,8},{7,9},{8,10},{9,11},{10,... | collective-permute-start | bytes 1572872 | tf_op jit(solution)/shard_map/ppermute | solution.py:21
  20.7 29.3 %collective-permute-start.3 = (bf16[16,128,128]{2,1,0:T(8,128)(2,1)}, bf16[16,128,128]{2,1,0:T(8,128)(2,1)S(1)}, u32[]{:S(2)}, u32[]{:S(2)}) collective-permute-start(bf16[16,128,128]{2,1,0:T(8,128)(2,1)} %gather_fusion.3), channel_id=1, source_target_pairs={{2,0},{3,1},{4,2},{5,3},{6,4},{7,5},{8,6},{9,7},{10,8},{11,9},{12,... | collective-permute-start | bytes 1572872 | tf_op jit(solution)/shard_map/ppermute | solution.py:21
  62.6 5.1 copy-start.20
  99.2 5.1 copy-start.19
  104.2 4.6 copy-start.7
  104.2 5.5 copy-start.8
  109.7 8.8 %copy-start.5 = (bf16[8192,128]{1,0:T(8,128)(2,1)S(1)}, bf16[8192,128]{1,0:T(8,128)(2,1)}, u32[]{:S(2)}) copy-start(bf16[8192,128]{1,0:T(8,128)(2,1)} %param.9) | copy-start | bytes 6291460
  118.6 14.0 %copy-start.24 = (s32[2,2048]{1,0:T(2,128)S(1)}, s32[2,2048]{1,0:T(2,128)}, u32[]{:S(2)}) copy-start(s32[2,2048]{1,0:T(2,128)} %param.15) | copy-start | bytes 49156
  124.4 23.8 %collective-permute-start.4 = (bf16[16,128,128]{2,1,0:T(8,128)(2,1)}, bf16[16,128,128]{2,1,0:T(8,128)(2,1)S(1)}, u32[]{:S(2)}, u32[]{:S(2)}) collective-permute-start(bf16[16,128,128]{2,1,0:T(8,128)(2,1)} %gather_fusion.11), channel_id=1, source_target_pairs={{0,1},{1,2},{2,3},{3,4},{4,5},{5,6},{6,7},{7,8},{8,9},{9,10},{10,1... | collective-permute-start | bytes 1572872 | tf_op jit(solution)/shard_map/ppermute | solution.py:21
  127.7 23.5 %collective-permute-start.5 = (bf16[16,128,128]{2,1,0:T(8,128)(2,1)}, bf16[16,128,128]{2,1,0:T(8,128)(2,1)}, u32[]{:S(2)}, u32[]{:S(2)}) collective-permute-start(bf16[16,128,128]{2,1,0:T(8,128)(2,1)} %gather_fusion.12), channel_id=1, source_target_pairs={{1,0},{2,1},{3,2},{4,3},{5,4},{6,5},{7,6},{8,7},{9,8},{10,9},{11,1... | collective-permute-start | bytes 1572872 | tf_op jit(solution)/shard_map/ppermute | solution.py:21
  134.1 19.1 %collective-permute-start.6 = (bf16[16,128,128]{2,1,0:T(8,128)(2,1)}, bf16[16,128,128]{2,1,0:T(8,128)(2,1)}, u32[]{:S(2)}, u32[]{:S(2)}) collective-permute-start(bf16[16,128,128]{2,1,0:T(8,128)(2,1)} %gather_fusion.13), channel_id=1, source_target_pairs={{0,2},{1,3},{2,4},{3,5},{4,6},{5,7},{6,8},{7,9},{8,10},{9,11},{10,... | collective-permute-start | bytes 1572872 | tf_op jit(solution)/shard_map/ppermute | solution.py:21
  139.0 28.1 %collective-permute-start.7 = (bf16[16,128,128]{2,1,0:T(8,128)(2,1)}, bf16[16,128,128]{2,1,0:T(8,128)(2,1)S(1)}, u32[]{:S(2)}, u32[]{:S(2)}) collective-permute-start(bf16[16,128,128]{2,1,0:T(8,128)(2,1)} %gather_fusion.14), channel_id=1, source_target_pairs={{2,0},{3,1},{4,2},{5,3},{6,4},{7,5},{8,6},{9,7},{10,8},{11,9},{12,... | collective-permute-start | bytes 1572872 | tf_op jit(solution)/shard_map/ppermute | solution.py:21
  194.0 18.6 %slice-start.2 = ((s8[14680064]{0:T(1024)(128)(4,1)}), s8[2097152]{0:T(1024)(128)(4,1)S(1)}, s32[]{:S(2)}) async-start(s8[14680064]{0:T(1024)(128)(4,1)} %bitcast.199), calls=%async_computation.3 | async-start | bytes 4194304
  198.6 5.0 copy-start.17
  198.6 14.1 %slice-start.3 = ((s8[14680064]{0:T(1024)(128)(4,1)}), s8[4194304]{0:T(1024)(128)(4,1)S(1)}, s32[]{:S(2)}) async-start(s8[14680064]{0:T(1024)(128)(4,1)} %bitcast.199), calls=%async_computation.4 | async-start | bytes 8388608
  203.6 4.5 copy-start.16
  203.6 9.1 %slice-start.4 = ((s8[14680064]{0:T(1024)(128)(4,1)}), s8[4194304]{0:T(1024)(128)(4,1)S(1)}, s32[]{:S(2)}) async-start(s8[14680064]{0:T(1024)(128)(4,1)} %bitcast.199), calls=%async_computation.5 | async-start | bytes 8388608
  208.1 4.6 slice-start.5
  208.1 4.6 copy-start.14
  241.7 23.8 %collective-permute-start.8 = (bf16[16,128,128]{2,1,0:T(8,128)(2,1)}, bf16[16,128,128]{2,1,0:T(8,128)(2,1)S(1)}, u32[]{:S(2)}, u32[]{:S(2)}) collective-permute-start(bf16[16,128,128]{2,1,0:T(8,128)(2,1)} %gather_fusion.22), channel_id=1, source_target_pairs={{0,1},{1,2},{2,3},{3,4},{4,5},{5,6},{6,7},{7,8},{8,9},{9,10},{10,1... | collective-permute-start | bytes 1572872 | tf_op jit(solution)/shard_map/ppermute | solution.py:21
  245.1 26.1 %collective-permute-start.9 = (bf16[16,128,128]{2,1,0:T(8,128)(2,1)}, bf16[16,128,128]{2,1,0:T(8,128)(2,1)}, u32[]{:S(2)}, u32[]{:S(2)}) collective-permute-start(bf16[16,128,128]{2,1,0:T(8,128)(2,1)} %gather_fusion.23), channel_id=1, source_target_pairs={{1,0},{2,1},{3,2},{4,3},{5,4},{6,5},{7,6},{8,7},{9,8},{10,9},{11,1... | collective-permute-start | bytes 1572872 | tf_op jit(solution)/shard_map/ppermute | solution.py:21
  252.3 20.7 %collective-permute-start.10 = (bf16[16,128,128]{2,1,0:T(8,128)(2,1)}, bf16[16,128,128]{2,1,0:T(8,128)(2,1)}, u32[]{:S(2)}, u32[]{:S(2)}) collective-permute-start(bf16[16,128,128]{2,1,0:T(8,128)(2,1)} %gather_fusion.24), channel_id=1, source_target_pairs={{0,2},{1,3},{2,4},{3,5},{4,6},{5,7},{6,8},{7,9},{8,10},{9,11},{10,... | collective-permute-start | bytes 1572872 | tf_op jit(solution)/shard_map/ppermute | solution.py:21
  255.7 28.3 %collective-permute-start.11 = (bf16[16,128,128]{2,1,0:T(8,128)(2,1)}, bf16[16,128,128]{2,1,0:T(8,128)(2,1)S(1)}, u32[]{:S(2)}, u32[]{:S(2)}) collective-permute-start(bf16[16,128,128]{2,1,0:T(8,128)(2,1)} %gather_fusion.25), channel_id=1, source_target_pairs={{2,0},{3,1},{4,2},{5,3},{6,4},{7,5},{8,6},{9,7},{10,8},{11,9},{12,... | collective-permute-start | bytes 1572872 | tf_op jit(solution)/shard_map/ppermute | solution.py:21
  310.9 18.6 %slice-start.6 = ((s8[14680064]{0:T(1024)(128)(4,1)}), s8[2097152]{0:T(1024)(128)(4,1)S(1)}, s32[]{:S(2)}) async-start(s8[14680064]{0:T(1024)(128)(4,1)} %bitcast.201), calls=%async_computation.7 | async-start | bytes 4194304
  315.4 5.1 copy-start.18
  315.4 14.2 %slice-start.7 = ((s8[14680064]{0:T(1024)(128)(4,1)}), s8[4194304]{0:T(1024)(128)(4,1)S(1)}, s32[]{:S(2)}) async-start(s8[14680064]{0:T(1024)(128)(4,1)} %bitcast.201), calls=%async_computation.8 | async-start | bytes 8388608
  320.4 4.6 copy-start.13
  320.5 9.1 %slice-start.8 = ((s8[14680064]{0:T(1024)(128)(4,1)}), s8[4194304]{0:T(1024)(128)(4,1)S(1)}, s32[]{:S(2)}) async-start(s8[14680064]{0:T(1024)(128)(4,1)} %bitcast.201), calls=%async_computation.9 | async-start | bytes 8388608
  367.9 52.0 %all-to-all-start = ((bf16[64,128,128]{2,1,0:T(8,128)(2,1)}), bf16[64,128,128]{2,1,0:T(8,128)(2,1)}, u32[]{:S(2)}, u32[]{:S(2)}) async-start(bf16[64,128,128]{2,1,0:T(8,128)(2,1)} %scatter_fusion), calls=%async_computation | async-start | bytes 4194304 | tf_op jit(solution)/shard_map/all_to_all | solution.py:136
  422.5 65.4 %copy-start.4 = (bf16[64,128,128]{2,1,0:T(8,128)(2,1)}, bf16[64,128,128]{2,1,0:T(8,128)(2,1)S(1)}, u32[]{:S(2)}) copy-start(bf16[64,128,128]{2,1,0:T(8,128)(2,1)S(1)} %gather_fusion.33) | copy-start | bytes 6291460
  422.5 8.2 %copy-start.6 = (bf16[16,4,128,128]{3,2,1,0:T(8,128)(2,1)S(1)}, bf16[16,4,128,128]{3,2,1,0:T(8,128)(2,1)}, u32[]{:S(2)}) copy-start(bf16[16,4,128,128]{3,2,1,0:T(8,128)(2,1)} %param.16) | copy-start | bytes 6291460
  424.0 14.1 %copy-start.22 = (s32[6,16,4,128]{3,2,1,0:T(4,128)S(1)}, s32[6,16,4,128]{3,2,1,0:T(4,128)}, u32[]{:S(2)}) copy-start(s32[6,16,4,128]{3,2,1,0:T(4,128)} %param.17) | copy-start | bytes 589828
  424.0 4.6 collective-permute-start.12
  427.3 3.4 collective-permute-start.13
  431.1 49.8 %collective-permute-start.14 = (bf16[2,18,1,128,128]{4,3,2,1,0:T(8,128)(2,1)S(1)}, bf16[2,18,1,128,128]{4,3,2,1,0:T(8,128)(2,1)S(1)}, u32[]{:S(2)}, u32[]{:S(2)}) collective-permute-start(bf16[2,18,1,128,128]{4,3,2,1,0:T(8,128)(2,1)S(1)} %get-tuple-element.9), channel_id=1, source_target_pairs={{0,1},{1,2},{2,3},{3,4},{4,5},{5,6},{6,7},{8,9},{9,10},{10,11},{11... | collective-permute-start | bytes 3538952 | tf_op jit(solution)/shard_map/ppermute | solution.py:31
  433.0 54.9 %collective-permute-start.15 = (bf16[2,18,1,128,128]{4,3,2,1,0:T(8,128)(2,1)S(1)}, bf16[2,18,1,128,128]{4,3,2,1,0:T(8,128)(2,1)S(1)}, u32[]{:S(2)}, u32[]{:S(2)}) collective-permute-start(bf16[2,18,1,128,128]{4,3,2,1,0:T(8,128)(2,1)S(1)} %get-tuple-element.10), channel_id=1, source_target_pairs={{1,0},{2,1},{3,2},{4,3},{5,4},{6,5},{7,6},{9,8},{10,9},{11,10},{12... | collective-permute-start | bytes 3538952 | tf_op jit(solution)/shard_map/ppermute | solution.py:32
  496.5 7.4 %copy-start.1 = (f32[18,6,128,128]{3,2,1,0:T(8,128)}, f32[18,6,128,128]{3,2,1,0:T(8,128)S(1)}, u32[]{:S(2)}) copy-start(f32[18,6,128,128]{3,2,1,0:T(8,128)S(1)} %get-tuple-element.8) | copy-start | bytes 21233668
  534.0 3.3 collective-permute-start.16
  536.1 3.2 collective-permute-start.17
  539.3 36.9 %slice-start = ((s8[7077888]{0:T(1024)(128)(4,1)}), s8[4194304]{0:T(1024)(128)(4,1)S(1)}, s32[]{:S(2)}) async-start(s8[7077888]{0:T(1024)(128)(4,1)} %bitcast.197), calls=%async_computation.1 | async-start | bytes 8388608
  539.5 26.1 %collective-permute-start.18 = (bf16[18,1,128,128]{3,2,1,0:T(8,128)(2,1)S(1)}, bf16[18,1,128,128]{3,2,1,0:T(8,128)(2,1)S(1)}, u32[]{:S(2)}, u32[]{:S(2)}) collective-permute-start(bf16[18,1,128,128]{3,2,1,0:T(8,128)(2,1)S(1)} %get-tuple-element.13), channel_id=1, source_target_pairs={{0,1},{1,2},{2,3},{3,4},{4,5},{5,6},{6,7},{8,9},{9,10},{10,11},{11... | collective-permute-start | bytes 1769480 | tf_op jit(solution)/shard_map/ppermute | solution.py:31
  541.7 34.5 %slice-start.1 = ((s8[7077888]{0:T(1024)(128)(4,1)}), s8[2883584]{0:T(1024)(128)(4,1)S(1)}, s32[]{:S(2)}) async-start(s8[7077888]{0:T(1024)(128)(4,1)} %bitcast.197), calls=%async_computation.2 | async-start | bytes 5767168
  541.7 29.6 %collective-permute-start.19 = (bf16[18,1,128,128]{3,2,1,0:T(8,128)(2,1)S(1)}, bf16[18,1,128,128]{3,2,1,0:T(8,128)(2,1)S(1)}, u32[]{:S(2)}, u32[]{:S(2)}) collective-permute-start(bf16[18,1,128,128]{3,2,1,0:T(8,128)(2,1)S(1)} %get-tuple-element.14), channel_id=1, source_target_pairs={{1,0},{2,1},{3,2},{4,3},{5,4},{6,5},{7,6},{9,8},{10,9},{11,10},{12... | collective-permute-start | bytes 1769480 | tf_op jit(solution)/shard_map/ppermute | solution.py:32
  (9 other events, 32.8 us)
where the time goes:
time: 613 us; the launch traced here: 602 us
  waiting for transfers between devices  181 us (30%)
  local copies, waits for them, and re-layouts  154 us (25%)
  matrix products  107 us (17%)
  other arithmetic  91 us (15%)
  starting transfers between devices  67.3 us (11%)
    dot_general x21, matrix products, local(): jnp.einsum('bij,bjr->bir', conductance[:, tile_k], chosen, preferred_elem...  107 us
    gather x21, local copies, waits for them, and re-layouts, local(): chosen = apply_extended[pattern[:, tile_k]]  90.1 us
    ppermute x4, waiting for transfers between devices, with_halo(): before = lax.ppermute(last, axis, up)  61.5 us
    ppermute x12, waiting for transfers between devices, passed_along(): lax.ppermute(value, axis, [(source, source + steps) for source in range(l...  55.9 us
    all_to_all x1, waiting for transfers between devices, local(): lax.all_to_all(outgoing, ('row', 'col'), split_axis=0, concat_axis=0, til...  46.7 us
    ppermute x12, starting transfers between devices, passed_along(): lax.ppermute(value, axis, [(source, source + steps) for source in range(l...  40.3 us
    convert_element_type x1, other arithmetic, local(): volume_dilatation.astype(jnp.bfloat16)  30 us
    convert_element_type x1, other arithmetic, local(): moved = (moving + STEP_SIZE * force).astype(jnp.bfloat16)  25.6 us
  transfers between devices with their start and end apart: 21, of which 16 were waited for; matrix products, arithmetic and copies ran while one was open for 5% of the time, Pallas kernels for 0%

commit v1 on v0

v1 whole, which is shorter than its diff:
```python
import functools

import jax
import jax.numpy as jnp
from jax import lax
from jax.experimental import pallas as pl
from jax.experimental.pallas import tpu as pltpu
from jax.sharding import PartitionSpec as P

ITERS = 3
LOWER = 1.0
UPPER = 10.0
ALPHA_T = 0.5
BOND_STIFFNESS = 1.0
STATE_STIFFNESS = 2.0
STEP_SIZE = 0.1
GHOST_STEPS = (1, -1, 2, -2)
SEND_ORDER = (2, 3, 0, 1)
MESH = pl.DeviceIdType.MESH
MIB = 1024 * 1024


def chebyshev_weights(count):
    center = (UPPER + LOWER) / 2.0
    half_width = (UPPER - LOWER) / 2.0
    ratio_value = center / half_width
    previous = 1.0 / ratio_value
    weights = []
    for step_number in range(count):
        current = 1.0 / (2.0 * ratio_value - previous)
        weights.append((current * previous, 2.0 * current / half_width))
        previous = current
    return (1.0 / center, weights)


def chebyshev_kernel(
    pattern,
    send_list,
    route,
    heat,
    active,
    diagonal,
    conductance,
    out,
    tiles,
    ext0,
    ext1,
    ext2,
    masked,
    outgoing,
    residual,
    direction,
    total,
    active_wide,
    diagonal_wide,
    tile_sem,
    send_sem,
    recv_sem,
):
    rows, cols = lax.axis_size("row"), lax.axis_size("col")
    devices = rows * cols
    me = lax.axis_index("row") * cols + lax.axis_index("col")
    blocks, length, cases = heat.shape
    tile_count = tiles.shape[1]
    cap = outgoing.shape[0] // len(GHOST_STEPS)
    exts = (ext0, ext1, ext2)
    first_scale, weights = chebyshev_weights(ITERS)

    tile_copy = pltpu.make_async_copy(conductance, tiles, tile_sem)
    tile_copy.start()

    def inside(index):
        return jnp.logical_and(index >= 0, index < devices)

    def place(index):
        return (lax.div(index, cols), lax.rem(index, cols))

    barrier = pltpu.get_barrier_semaphore()
    for step in GHOST_STEPS:

        @pl.when(inside(me + step))
        def _():
            pl.semaphore_signal(barrier, inc=1, device_id=place(me + step), device_id_type=MESH)

    def ghost_copy(it, group):
        return pltpu.make_async_remote_copy(
            src_ref=outgoing.at[pl.ds(group * cap, cap)],
            dst_ref=exts[it].at[pl.ds(blocks + group * cap, cap)],
            send_sem=send_sem.at[it, group],
            recv_sem=recv_sem.at[it, group],
            device_id=place(me + GHOST_STEPS[group]),
            device_id_type=MESH,
        )

    wide = jnp.concatenate([active[...], diagonal[...]], axis=0).T
    for b in range(blocks):
        column = jnp.broadcast_to(wide[:, b : b + 1], (length, cases))
        active_wide[b] = column.astype(jnp.bfloat16)

    @pl.loop(0, blocks)
    def _(b):
        source = heat[b].astype(jnp.float32)
        start = source * first_scale
        residual[b] = source
        direction[b] = start
        value = (start * active_wide[b].astype(jnp.float32)).astype(jnp.bfloat16)
        masked[b] = value
        ext0[b] = value

    peers = sum(jnp.where(inside(me + step), 1, 0) for step in GHOST_STEPS)
    pl.semaphore_wait(barrier, peers)

    for it in range(ITERS):
        ext = exts[it]
        for group in SEND_ORDER:
            step = GHOST_STEPS[group]
            if it > 0:

                @pl.when(inside(me + step))
                def _():
                    ghost_copy(it - 1, group).wait_send()

            @pl.loop(0, cap)
            def _(j):
                outgoing[group * cap + j] = masked[send_list[group * cap + j]]

            @pl.when(inside(me + step))
            def _():
                ghost_copy(it, group).start()

        for group, step in enumerate(GHOST_STEPS):

            @pl.when(jnp.logical_not(inside(me - step)))
            def _():
                ext[pl.ds(blocks + group * cap, cap)] = jnp.zeros(
                    (cap, length, cases), jnp.bfloat16
                )

        if it == 0:
            for b in range(blocks):
                diagonal_wide[b] = jnp.broadcast_to(
                    wide[:, blocks + b : blocks + b + 1], (length, cases)
                )
            tile_copy.wait()

        @pl.loop(0, blocks)
        def _(b):
            own = jnp.dot(tiles[b, 0], masked[b], preferred_element_type=jnp.float32)
            held = direction[b]
            residual[b] = (
                residual[b] - diagonal_wide[b] * held - active_wide[b].astype(jnp.float32) * own
            )
            if it == 0:
                total[b] = held
            else:
                total[b] = total[b] + held

        for group, step in enumerate(GHOST_STEPS):

            @pl.when(inside(me - step))
            def _():
                ghost_copy(it, group).wait_recv()

        old_weight, res_weight = weights[it]
        unroll = 2

        @pl.loop(0, blocks // unroll)
        def _(pair):
            for part in range(unroll):
                b = pair * unroll + part
                chosen = [ext[blocks + b]]
                for k in range(2, tile_count):
                    chosen.append(ext[pattern[b * tile_count + k]])
                row = jnp.concatenate([tiles[b, k] for k in range(1, tile_count)], axis=1)
                far = jnp.dot(
                    row, jnp.concatenate(chosen, axis=0), preferred_element_type=jnp.float32
                )
                mask = active_wide[b].astype(jnp.float32)
                left = residual[b] - mask * far
                held = old_weight * direction[b] + res_weight * left
                if it < ITERS - 1:
                    residual[b] = left
                    direction[b] = held
                    value = (held * mask).astype(jnp.bfloat16)
                    masked[b] = value
                    exts[it + 1][b] = value
                else:
                    masked[b] = (total[b] + held).astype(jnp.bfloat16)

    @pl.loop(0, out.shape[0])
    def _(j):
        out[j] = masked[route[j]]

    for group, step in enumerate(GHOST_STEPS):

        @pl.when(inside(me + step))
        def _():
            ghost_copy(ITERS - 1, group).wait_send()


def chebyshev(pattern, send_list, route, heat, active, diagonal, conductance):
    blocks, length, cases = heat.shape
    tile_count = conductance.shape[1]
    ghosts = send_list.shape[0]
    smem = pl.BlockSpec(memory_space=pltpu.SMEM)
    vmem = pl.BlockSpec(memory_space=pltpu.VMEM)
    hbm = pl.BlockSpec(memory_space=pl.ANY)
    state = pltpu.VMEM((blocks, length, cases), jnp.float32)
    ext = pltpu.VMEM((blocks + ghosts, length, cases), jnp.bfloat16)
    half = pltpu.VMEM((blocks, length, cases), jnp.bfloat16)
    return pl.pallas_call(
        chebyshev_kernel,
        out_shape=jax.ShapeDtypeStruct((route.shape[0], length, cases), jnp.bfloat16),
        in_specs=[smem, smem, smem, vmem, vmem, vmem, hbm],
        out_specs=vmem,
        scratch_shapes=[
            pltpu.VMEM(conductance.shape, jnp.bfloat16),
            ext,
            ext,
            ext,
            half,
            pltpu.VMEM((ghosts, length, cases), jnp.bfloat16),
            state,
            state,
            state,
            half,
            state,
            pltpu.SemaphoreType.DMA,
            pltpu.SemaphoreType.DMA((ITERS, len(GHOST_STEPS))),
            pltpu.SemaphoreType.DMA((ITERS, len(GHOST_STEPS))),
        ],
        compiler_params=pltpu.CompilerParams(
            collective_id=0, has_side_effects=True, vmem_limit_bytes=58 * MIB
        ),
        name="chebyshev",
    )(pattern, send_list, route, heat, active, diagonal, conductance)


def edges(field, axis, dim):
    size, length = lax.axis_size(axis), field.shape[dim]
    up = [(i, i + 1) for i in range(size - 1)]
    down = [(j, i) for i, j in up]
    last = lax.slice_in_dim(field, length - 1, length, axis=dim)
    leading = lax.slice_in_dim(field, 0, 1, axis=dim)
    return lax.ppermute(last, axis, up), lax.ppermute(leading, axis, down)


def bond_sum(field, live):
    sent = field.astype(jnp.bfloat16)
    low_x, high_x = edges(sent, "row", 0)
    low_y, high_y = edges(sent, "col", 1)
    wide_x = jnp.concatenate([low_x.astype(jnp.float32), field, high_x.astype(jnp.float32)], 0)
    wide_y = jnp.concatenate([low_y.astype(jnp.float32), field, high_y.astype(jnp.float32)], 1)
    wide_z = jnp.pad(field, ((0, 0), (0, 0), (1, 1), (0, 0)))
    return (
        live[0] * wide_x[2:]
        + live[1] * wide_y[:, 2:]
        + live[2] * wide_z[:, :, 2:]
        + live[3] * wide_x[:-2]
        + live[4] * wide_y[:, :-2]
        + live[5] * wide_z[:, :, :-2]
    )


def local(
    heat_source,
    diagonal,
    active,
    conductance,
    pattern,
    send_list,
    owner_map,
    displacement,
    bond_live,
):
    blocks, tile_count, length = conductance.shape[:3]
    cases = heat_source.shape[1]
    devices = lax.axis_size(("row", "col"))
    me = lax.axis_index(("row", "col"))
    cap = max(1, blocks // devices)

    slots = jnp.arange(blocks, dtype=jnp.int32)
    mine = lax.dynamic_slice_in_dim(owner_map, me * blocks, blocks, axis=1)
    my_distance = (mine[0] - me + devices) % devices
    of_slot = mine[1][None, :] == slots[:, None]
    block_of = jnp.sum(jnp.where(of_slot, slots[None, :], 0), axis=1)
    distance = jnp.sum(jnp.where(of_slot, my_distance[None, :], 0), axis=1)
    rank = jnp.sum(
        ((distance[:, None] == distance[None, :]) & (slots[None, :] < slots[:, None])).astype(
            jnp.int32
        ),
        axis=1,
    )
    target = ((me + distance) % devices) * cap + rank
    places = jnp.arange(devices * cap, dtype=jnp.int32)
    route = jnp.sum(jnp.where(target[None, :] == places[:, None], block_of[None, :], 0), axis=1)
    source_row = ((me - distance + devices) % devices) * cap + rank

    outgoing = chebyshev(
        pattern.reshape(-1),
        send_list.reshape(-1),
        route,
        heat_source.reshape(blocks, length, cases),
        active.astype(jnp.float32).reshape(blocks, length),
        diagonal.reshape(blocks, length),
        conductance,
    )
    arrived = lax.all_to_all(outgoing, ("row", "col"), split_axis=0, concat_axis=0, tiled=True)
    bricks = arrived[source_row].reshape(displacement.shape)

    live = bond_live.astype(jnp.float32)[..., None]
    count = jnp.sum(live, axis=0)
    moving = displacement.astype(jnp.float32)
    heat = (ALPHA_T * 0.5) * bricks.astype(jnp.float32)
    dilatation = (bond_sum(moving - heat, live) - count * (moving + heat)) / 6.0
    force = BOND_STIFFNESS * 6.0 * dilatation + STATE_STIFFNESS * (
        bond_sum(dilatation, live) - count * dilatation
    )
    moved = (moving + STEP_SIZE * force).astype(jnp.bfloat16)
    return (bricks, moved)


def solution(mesh):
    return jax.shard_map(
        local,
        mesh=mesh,
        in_specs=(
            P(("row", "col"), None),
            P(("row", "col")),
            P(("row", "col")),
            P(("row", "col"), None, None, None),
            P(("row", "col"), None),
            P(("row", "col"), None, None),
            P(),
            P("row", "col", None, None),
            P(None, "row", "col", None),
        ),
        out_specs=(P("row", "col", None, None), P("row", "col", None, None)),
        check_vma=False,
    )
```

time: 613 us -> 280 us (0.46); the launches traced: 602 us -> 276 us
  local copies, waits for them, and re-layouts: 154 us -> 6.41 us
  Pallas kernels: 0 us -> 123 us
  matrix products: 107 us -> 0 us
  waiting for transfers between devices: 181 us -> 77.9 us
  other arithmetic: 91 us -> 27.1 us
  starting transfers between devices: 67.3 us -> 41 us
    pallas_call x0 -> x1, Pallas kernels: none -> 123 us  [chebyshev(): pl.pallas_call(chebyshev_kernel, out_shape=jax.ShapeDtypeStruct((route.sh...]
    dot_general x21 -> x0, matrix products: 107 us -> none  [local(): jnp.einsum('bij,bjr->bir', conductance[:, tile_k], chosen, preferred_elem...]
    gather x34 -> x1, local copies, waits for them, and re-layouts: 110 us -> 2.54 us  [local(): bricks = arrived[source_row].reshape(displacement.shape)]
    ppermute x20 -> x8, waiting for transfers between devices: 134 us -> 30.9 us  [edges(): return (lax.ppermute(last, axis, up), lax.ppermute(leading, axis, down))]
    convert_element_type x9 -> x11, other arithmetic: 56.5 us -> 13.4 us  [the longest x2 12.8 us: bond_sum(): sent = field.astype(jnp.bfloat16)]
    ppermute x20 -> x8, starting transfers between devices: 62.4 us -> 22.9 us  [edges(): return (lax.ppermute(last, axis, up), lax.ppermute(leading, axis, down))]
    unnamed x84 -> x9, local copies, waits for them, and re-layouts: 23.2 us -> 1.51 us
    convert_element_type x1, other arithmetic: 25.6 us -> 10.6 us  [local(): moved = (moving + STEP_SIZE * force).astype(jnp.bfloat16)]
  transfers between devices with their start and end apart: 21 -> 9, of which waited for: 16 -> 5; matrix products, arithmetic and copies ran while one was open for 5% -> 0% of each run, Pallas kernels for 0% -> 0%
where the time goes in v1:
time: 280 us; the launch traced here: 276 us
  Pallas kernels  123 us (44%)
  waiting for transfers between devices  77.9 us (28%)
  starting transfers between devices  41 us (15%)
  other arithmetic  27.1 us (10%)
  local copies, waits for them, and re-layouts  6.41 us (2%)
    pallas_call x1, Pallas kernels, chebyshev(): pl.pallas_call(chebyshev_kernel, out_shape=jax.ShapeDtypeStruct((route.sh...  123 us
    all_to_all x1, waiting for transfers between devices, local(): lax.all_to_all(outgoing, ('row', 'col'), split_axis=0, concat_axis=0, til...  46.9 us
    ppermute x8, waiting for transfers between devices, edges(): return (lax.ppermute(last, axis, up), lax.ppermute(leading, axis, down))  30.9 us
    ppermute x8, starting transfers between devices, edges(): return (lax.ppermute(last, axis, up), lax.ppermute(leading, axis, down))  22.9 us
    all_to_all x1, starting transfers between devices, local(): lax.all_to_all(outgoing, ('row', 'col'), split_axis=0, concat_axis=0, til...  18.1 us
    convert_element_type x2, other arithmetic, bond_sum(): sent = field.astype(jnp.bfloat16)  12.8 us
    convert_element_type x1, other arithmetic, local(): moved = (moving + STEP_SIZE * force).astype(jnp.bfloat16)  10.6 us
  transfers between devices with their start and end apart: 9, of which 5 were waited for; matrix products, arithmetic and copies ran while one was open for 0% of the time, Pallas kernels for 0%

profile of v1, /device:TPU:8, one launch (start us, length us, event | category | flops | bytes accessed | tf_op | source)
XLA Modules:
  0.0 276.0 jit_solution(11074572789182204543)
XLA Ops:
  0.6 0.0 copy-start
  0.7 0.7 copy-done
  1.4 0.1 constant_dynamic-slice_fusion
  1.4 0.1 select_reduce_fusion.2
  1.6 0.2 convert_reduce_fusion
  1.8 0.8 copy.12
  2.5 0.7 reshape.129.pattern
  3.3 1.4 convert_bitcast_fusion.active
  4.6 1.3 reshape.130.send_list
  6.0 0.7 select_reduce_fusion.route
  6.7 122.7 %chebyshev.1 = bf16[64,128,128]{2,1,0:T(8,128)(2,1)} custom-call(s32[448]{0:T(512)} %reshape.129.pattern, s32[64]{0:T(128)} %reshape.130.send_list, s32[64]{0:T(128)} %select_reduce_fusion.route, bf16[64,128,128]{2,1,0:T(8,128)(2,1)} %bitcast.34, f32[64,128]{1,0:T(8,128)} %convert_bitcast_fusion.active, f32[64,128]{1,0:T(8,128)} %bitcast.35, ...), custom_call_target="tpu_custom_call" | custom-call | tf_op jit(solution)/shard_map/chebyshev/pallas_call | solution.py:211
  129.3 0.0 copy-start.3
  129.3 18.1 %all-to-all-start = ((bf16[64,128,128]{2,1,0:T(8,128)(2,1)}), bf16[64,128,128]{2,1,0:T(8,128)(2,1)}, u32[]{:S(2)}, u32[]{:S(2)}) async-start(bf16[64,128,128]{2,1,0:T(8,128)(2,1)} %chebyshev.1), calls=%async_computation | async-start | bytes 4194304 | tf_op jit(solution)/shard_map/all_to_all | solution.py:308
  147.5 0.0 copy-done.3
  147.6 46.9 %all-to-all-done = bf16[64,128,128]{2,1,0:T(8,128)(2,1)} async-done(((bf16[64,128,128]{2,1,0:T(8,128)(2,1)}), bf16[64,128,128]{2,1,0:T(8,128)(2,1)}, u32[]{:S(2)}, u32[]{:S(2)}) %all-to-all-start) | async-done | bytes 2097184 | tf_op jit(solution)/shard_map/all_to_all | solution.py:308
  194.5 2.5 gather_fusion
  197.1 0.0 copy-start.1
  197.1 3.2 %fusion.40 = (bf16[16,4,128,128]{3,2,1,0:T(8,128)(2,1)S(1)}, f32[16,4,128,128]{3,2,1,0:T(8,128)S(1)}) fusion(bf16[16,4,128,128]{3,2,1,0:T(8,128)(2,1)S(1)} %bitcast.31, bf16[16,4,128,128]{3,2,1,0:T(8,128)(2,1)} %param.16), kind=kLoop, calls=%fused_computation.87 | loop fusion | flops 5242880 | bytes 10485760 | tf_op jit(solution)/shard_map/convert_element_type | solution.py:249
  200.3 0.0 copy-start.2
  200.3 0.1 fusion.45
  200.4 4.9 %collective-permute-start.1 = (bf16[16,1,128,128]{3,2,1,0:T(8,128)(2,1)S(1)}, bf16[16,1,128,128]{3,2,1,0:T(8,128)(2,1)S(1)}, u32[]{:S(2)}, u32[]{:S(2)}) collective-permute-start(bf16[16,1,128,128]{3,2,1,0:T(8,128)(2,1)S(1)} %get-tuple-element.14), channel_id=1, source_target_pairs={{1,0},{2,1},{3,2},{4,3},{5,4},{6,5},{7,6},{9,8},{10,9},{11,10},{12... | collective-permute-start | bytes 1572872 | tf_op jit(solution)/shard_map/ppermute | solution.py:245
  205.3 1.9 collective-permute-start.3
  207.2 0.1 convert_reduce_fusion.1
  207.3 1.3 collective-permute-start
  208.6 3.0 %collective-permute-start.2 = (bf16[1,4,128,128]{3,2,1,0:T(8,128)(2,1)S(1)}, bf16[1,4,128,128]{3,2,1,0:T(8,128)(2,1)S(1)}, u32[]{:S(2)}, u32[]{:S(2)}) collective-permute-start(bf16[1,4,128,128]{3,2,1,0:T(8,128)(2,1)S(1)} %get-tuple-element.13), channel_id=1, source_target_pairs={{0,8},{8,16},{16,24},{1,9},{9,17},{17,25},{2,10},{10,18},{18,26},{... | collective-permute-start | bytes 393224 | tf_op jit(solution)/shard_map/ppermute | solution.py:245
  211.7 0.0 collective-permute-done
  211.7 0.9 collective-permute-done.2
  212.6 15.6 %collective-permute-done.1 = bf16[16,1,128,128]{3,2,1,0:T(8,128)(2,1)S(1)} collective-permute-done((bf16[16,1,128,128]{3,2,1,0:T(8,128)(2,1)S(1)}, bf16[16,1,128,128]{3,2,1,0:T(8,128)(2,1)S(1)}, u32[]{:S(2)}, u32[]{:S(2)}) %collective-permute-start.1) | collective-permute-done | bytes 524320 | tf_op jit(solution)/shard_map/ppermute | solution.py:245
  228.2 0.1 convert_element_type.58
  228.3 0.0 collective-permute-done.3
  228.3 0.1 convert_element_type.60
  228.4 0.0 copy-done.1
  228.5 0.0 copy-done.2
  228.5 9.6 %fusion.39 = (bf16[16,4,128,128]{3,2,1,0:T(8,128)(2,1)S(1)}, f32[16,4,128,128]{3,2,1,0:T(8,128)S(1)}) fusion(bf16[16,4,128,128]{3,2,1,0:T(8,128)(2,1)S(1)} %bitcast.32, bf16[16,4,128,128]{3,2,1,0:T(8,128)(2,1)S(1)} %copy-done.2, f32[16,4,128]{2,1,0:T(4,128)S(1)} %convert_reduce_fusion.1, f32[16,4,128]{2,1,0:T(4,128)S(1)} %get-tuple-element.17, ...), kind=kLoop, calls=%fused_computation.86 | loop fusion | flops 24117248 | bytes 17530880 | tf_op jit(solution)/shard_map/convert_element_type | solution.py:249
  238.1 0.1 fusion.43
  238.2 5.5 %collective-permute-start.5 = (bf16[16,1,128,128]{3,2,1,0:T(8,128)(2,1)S(1)}, bf16[16,1,128,128]{3,2,1,0:T(8,128)(2,1)S(1)}, u32[]{:S(2)}, u32[]{:S(2)}) collective-permute-start(bf16[16,1,128,128]{3,2,1,0:T(8,128)(2,1)S(1)} %get-tuple-element.10), channel_id=1, source_target_pairs={{1,0},{2,1},{3,2},{4,3},{5,4},{6,5},{7,6},{9,8},{10,9},{11,10},{12... | collective-permute-start | bytes 1572872 | tf_op jit(solution)/shard_map/ppermute | solution.py:245
  243.7 1.9 collective-permute-start.7
  245.7 1.3 collective-permute-start.4
  247.0 3.0 %collective-permute-start.6 = (bf16[1,4,128,128]{3,2,1,0:T(8,128)(2,1)S(1)}, bf16[1,4,128,128]{3,2,1,0:T(8,128)(2,1)S(1)}, u32[]{:S(2)}, u32[]{:S(2)}) collective-permute-start(bf16[1,4,128,128]{3,2,1,0:T(8,128)(2,1)S(1)} %get-tuple-element.9), channel_id=1, source_target_pairs={{0,8},{8,16},{16,24},{1,9},{9,17},{17,25},{2,10},{10,18},{18,26},{... | collective-permute-start | bytes 393224 | tf_op jit(solution)/shard_map/ppermute | solution.py:245
  250.0 0.7 broadcast_multiply_fusion
  250.8 0.0 collective-permute-done.4
  250.8 0.2 collective-permute-done.6
  251.0 14.2 %collective-permute-done.5 = bf16[16,1,128,128]{3,2,1,0:T(8,128)(2,1)S(1)} collective-permute-done((bf16[16,1,128,128]{3,2,1,0:T(8,128)(2,1)S(1)}, bf16[16,1,128,128]{3,2,1,0:T(8,128)(2,1)S(1)}, u32[]{:S(2)}, u32[]{:S(2)}) %collective-permute-start.5) | collective-permute-done | bytes 524320 | tf_op jit(solution)/shard_map/ppermute | solution.py:245
  265.3 0.1 convert_element_type.63
  265.4 0.0 collective-permute-done.7
  265.4 0.1 convert_element_type.65
  265.5 10.6 %fusion.28 = bf16[16,4,128,128]{3,2,1,0:T(8,128)(2,1)} fusion(f32[16,4,128,128]{3,2,1,0:T(8,128)S(1)} %get-tuple-element.5, f32[16,4,128,128]{3,2,1,0:T(8,128)S(1)} %broadcast_multiply_fusion, f32[16,1,128,128]{3,2,1,0:T(8,128)S(1)} %convert_element_type.65, f32[1,4,128,128]{3,2,1,0:T(8,128)S(1)} %convert_element_type.64, ...), kind=kLoop, calls=%fused_computation.45 | loop fusion | flops 24117248 | bytes 15433728 | tf_op jit(solution)/shard_map/convert_element_type | solution.py:319
  (13 shorter events, 0.2 us)
Async XLA Ops:
  0.6 0.7 copy-start
  129.3 18.1 %copy-start.3 = (s32[6,16,4,128]{3,2,1,0:T(4,128)S(1)}, s32[6,16,4,128]{3,2,1,0:T(4,128)}, u32[]{:S(2)}) copy-start(s32[6,16,4,128]{3,2,1,0:T(4,128)} %param.17) | copy-start | bytes 589828
  129.3 65.2 %all-to-all-start = ((bf16[64,128,128]{2,1,0:T(8,128)(2,1)}), bf16[64,128,128]{2,1,0:T(8,128)(2,1)}, u32[]{:S(2)}, u32[]{:S(2)}) async-start(bf16[64,128,128]{2,1,0:T(8,128)(2,1)} %chebyshev.1), calls=%async_computation | async-start | bytes 4194304 | tf_op jit(solution)/shard_map/all_to_all | solution.py:308
  197.1 31.4 %copy-start.1 = (bf16[64,128,128]{2,1,0:T(8,128)(2,1)}, bf16[64,128,128]{2,1,0:T(8,128)(2,1)S(1)}, u32[]{:S(2)}) copy-start(bf16[64,128,128]{2,1,0:T(8,128)(2,1)S(1)} %gather_fusion) | copy-start | bytes 6291460
  200.3 28.1 %copy-start.2 = (bf16[16,4,128,128]{3,2,1,0:T(8,128)(2,1)S(1)}, bf16[16,4,128,128]{3,2,1,0:T(8,128)(2,1)}, u32[]{:S(2)}) copy-start(bf16[16,4,128,128]{3,2,1,0:T(8,128)(2,1)} %param.16) | copy-start | bytes 6291460
  200.4 27.8 %collective-permute-start.1 = (bf16[16,1,128,128]{3,2,1,0:T(8,128)(2,1)S(1)}, bf16[16,1,128,128]{3,2,1,0:T(8,128)(2,1)S(1)}, u32[]{:S(2)}, u32[]{:S(2)}) collective-permute-start(bf16[16,1,128,128]{3,2,1,0:T(8,128)(2,1)S(1)} %get-tuple-element.14), channel_id=1, source_target_pairs={{1,0},{2,1},{3,2},{4,3},{5,4},{6,5},{7,6},{9,8},{10,9},{11,10},{12... | collective-permute-start | bytes 1572872 | tf_op jit(solution)/shard_map/ppermute | solution.py:245
  205.3 23.0 %collective-permute-start.3 = (bf16[16,1,128,128]{3,2,1,0:T(8,128)(2,1)S(1)}, bf16[16,1,128,128]{3,2,1,0:T(8,128)(2,1)S(1)}, u32[]{:S(2)}, u32[]{:S(2)}) collective-permute-start(bf16[16,1,128,128]{3,2,1,0:T(8,128)(2,1)S(1)} %get-tuple-element.15), channel_id=1, source_target_pairs={{0,1},{1,2},{2,3},{3,4},{4,5},{5,6},{6,7},{8,9},{9,10},{10,11},{11... | collective-permute-start | bytes 1572872 | tf_op jit(solution)/shard_map/ppermute | solution.py:245
  207.3 4.4 %collective-permute-start = (bf16[1,4,128,128]{3,2,1,0:T(8,128)(2,1)S(1)}, bf16[1,4,128,128]{3,2,1,0:T(8,128)(2,1)S(1)}, u32[]{:S(2)}, u32[]{:S(2)}) collective-permute-start(bf16[1,4,128,128]{3,2,1,0:T(8,128)(2,1)S(1)} %get-tuple-element.12), channel_id=1, source_target_pairs={{8,0},{16,8},{24,16},{9,1},{17,9},{25,17},{10,2},{18,10},{26,18},{... | collective-permute-start | bytes 393224 | tf_op jit(solution)/shard_map/ppermute | solution.py:245
  208.6 4.0 %collective-permute-start.2 = (bf16[1,4,128,128]{3,2,1,0:T(8,128)(2,1)S(1)}, bf16[1,4,128,128]{3,2,1,0:T(8,128)(2,1)S(1)}, u32[]{:S(2)}, u32[]{:S(2)}) collective-permute-start(bf16[1,4,128,128]{3,2,1,0:T(8,128)(2,1)S(1)} %get-tuple-element.13), channel_id=1, source_target_pairs={{0,8},{8,16},{16,24},{1,9},{9,17},{17,25},{2,10},{10,18},{18,26},{... | collective-permute-start | bytes 393224 | tf_op jit(solution)/shard_map/ppermute | solution.py:245
  238.2 27.1 %collective-permute-start.5 = (bf16[16,1,128,128]{3,2,1,0:T(8,128)(2,1)S(1)}, bf16[16,1,128,128]{3,2,1,0:T(8,128)(2,1)S(1)}, u32[]{:S(2)}, u32[]{:S(2)}) collective-permute-start(bf16[16,1,128,128]{3,2,1,0:T(8,128)(2,1)S(1)} %get-tuple-element.10), channel_id=1, source_target_pairs={{1,0},{2,1},{3,2},{4,3},{5,4},{6,5},{7,6},{9,8},{10,9},{11,10},{12... | collective-permute-start | bytes 1572872 | tf_op jit(solution)/shard_map/ppermute | solution.py:245
  243.7 21.6 %collective-permute-start.7 = (bf16[16,1,128,128]{3,2,1,0:T(8,128)(2,1)S(1)}, bf16[16,1,128,128]{3,2,1,0:T(8,128)(2,1)S(1)}, u32[]{:S(2)}, u32[]{:S(2)}) collective-permute-start(bf16[16,1,128,128]{3,2,1,0:T(8,128)(2,1)S(1)} %get-tuple-element.11), channel_id=1, source_target_pairs={{0,1},{1,2},{2,3},{3,4},{4,5},{5,6},{6,7},{8,9},{9,10},{10,11},{11... | collective-permute-start | bytes 1572872 | tf_op jit(solution)/shard_map/ppermute | solution.py:245
  245.7 5.1 %collective-permute-start.4 = (bf16[1,4,128,128]{3,2,1,0:T(8,128)(2,1)S(1)}, bf16[1,4,128,128]{3,2,1,0:T(8,128)(2,1)S(1)}, u32[]{:S(2)}, u32[]{:S(2)}) collective-permute-start(bf16[1,4,128,128]{3,2,1,0:T(8,128)(2,1)S(1)} %get-tuple-element.8), channel_id=1, source_target_pairs={{8,0},{16,8},{24,16},{9,1},{17,9},{25,17},{10,2},{18,10},{26,18},{... | collective-permute-start | bytes 393224 | tf_op jit(solution)/shard_map/ppermute | solution.py:245
  247.0 4.0 %collective-permute-start.6 = (bf16[1,4,128,128]{3,2,1,0:T(8,128)(2,1)S(1)}, bf16[1,4,128,128]{3,2,1,0:T(8,128)(2,1)S(1)}, u32[]{:S(2)}, u32[]{:S(2)}) collective-permute-start(bf16[1,4,128,128]{3,2,1,0:T(8,128)(2,1)S(1)} %get-tuple-element.9), channel_id=1, source_target_pairs={{0,8},{8,16},{16,24},{1,9},{9,17},{17,25},{2,10},{10,18},{18,26},{... | collective-permute-start | bytes 393224 | tf_op jit(solution)/shard_map/ppermute | solution.py:245

commit v2 on v1

--- a/solution.py
+++ b/solution.py
@@ -1,5 +1,3 @@
-import functools
-
 import jax
 import jax.numpy as jnp
 from jax import lax
@@ -236,30 +234,229 @@
     )(pattern, send_list, route, heat, active, diagonal, conductance)
 
 
-def edges(field, axis, dim):
-    size, length = lax.axis_size(axis), field.shape[dim]
-    up = [(i, i + 1) for i in range(size - 1)]
-    down = [(j, i) for i, j in up]
-    last = lax.slice_in_dim(field, length - 1, length, axis=dim)
-    leading = lax.slice_in_dim(field, 0, 1, axis=dim)
-    return lax.ppermute(last, axis, up), lax.ppermute(leading, axis, down)
-
-
-def bond_sum(field, live):
-    sent = field.astype(jnp.bfloat16)
-    low_x, high_x = edges(sent, "row", 0)
-    low_y, high_y = edges(sent, "col", 1)
-    wide_x = jnp.concatenate([low_x.astype(jnp.float32), field, high_x.astype(jnp.float32)], 0)
-    wide_y = jnp.concatenate([low_y.astype(jnp.float32), field, high_y.astype(jnp.float32)], 1)
-    wide_z = jnp.pad(field, ((0, 0), (0, 0), (1, 1), (0, 0)))
-    return (
-        live[0] * wide_x[2:]
-        + live[1] * wide_y[:, 2:]
-        + live[2] * wide_z[:, :, 2:]
-        + live[3] * wide_x[:-2]
-        + live[4] * wide_y[:, :-2]
-        + live[5] * wide_z[:, :, :-2]
-    )
+def mechanics_kernel(
+    source_row,
+    arrived,
+    displacement,
+    bond_live,
+    bricks,
+    moved,
+    stretch,
+    dilation,
+    live,
+    send_x,
+    send_y,
+    recv_x,
+    recv_y,
+    send_sem,
+    recv_sem,
+):
+    sizes = (lax.axis_size("row"), lax.axis_size("col"))
+    here = (lax.axis_index("row"), lax.axis_index("col"))
+    columns_x, columns_y, length, cases = displacement.shape
+    sends, recvs = ((send_x, send_y), (recv_x, recv_y))
+    bonds = ((0, 3), (1, 4))
+    quarter = ALPHA_T * 0.5
+
+    def beside(axis, side):
+        return here[axis] + (1 if side == 0 else -1)
+
+    def present(axis, side):
+        index = beside(axis, side)
+        return jnp.logical_and(index >= 0, index < sizes[axis])
+
+    def place(axis, side):
+        index = beside(axis, side)
+        return (index, here[1]) if axis == 0 else (here[0], index)
+
+    def edge_copy(turn, axis, side):
+        return pltpu.make_async_remote_copy(
+            src_ref=sends[axis].at[turn, side],
+            dst_ref=recvs[axis].at[turn, 1 - side],
+            send_sem=send_sem.at[turn, axis, side],
+            recv_sem=recv_sem.at[turn, axis, 1 - side],
+            device_id=place(axis, side),
+            device_id_type=MESH,
+        )
+
+    pairs = [(axis, side) for axis in (1, 0) for side in (0, 1)]
+    barrier = pltpu.get_barrier_semaphore()
+    for axis, side in pairs:
+
+        @pl.when(present(axis, side))
+        def _():
+            pl.semaphore_signal(barrier, inc=1, device_id=place(axis, side), device_id_type=MESH)
+
+    def fetch(x, y):
+        temperature = arrived[source_row[x * columns_y + y]]
+        bricks[x, y] = temperature
+        value = displacement[x, y].astype(jnp.float32) - quarter * temperature.astype(jnp.float32)
+        stretch[x + 1, y] = value
+        return value.astype(jnp.bfloat16)
+
+    def launch(turn, axis):
+        for side in (0, 1):
+
+            @pl.when(present(axis, side))
+            def _():
+                edge_copy(turn, axis, side).start()
+
+    def arrive(turn, axis, side, add):
+        @pl.when(present(axis, side))
+        def _():
+            edge_copy(turn, axis, 1 - side).wait_recv()
+            if axis == 0:
+                for y in range(columns_y):
+                    add(columns_x - 1 if side == 0 else 0, y, y)
+            else:
+
+                @pl.loop(0, columns_x)
+                def _(x):
+                    add(x, columns_y - 1 if side == 0 else 0, x)
+
+    def bond_sum(field, x, y):
+        middle = field[x + 1, y]
+        bond = [live[d, x * columns_y + y].astype(jnp.float32) for d in range(6)]
+        result = bond[0] * field[x + 2, y] + bond[3] * field[x, y]
+        result = result + bond[2] * pltpu.roll(middle, length - 1, 0)
+        result = result + bond[5] * pltpu.roll(middle, 1, 0)
+        if y + 1 < columns_y:
+            result = result + bond[1] * field[x + 1, y + 1]
+        if y > 0:
+            result = result + bond[4] * field[x + 1, y - 1]
+        count = bond[0] + bond[1] + bond[2] + bond[3] + bond[4] + bond[5]
+        return middle, result, count
+
+    @pl.loop(0, columns_x)
+    def _(x):
+        send_y[0, 0, x] = fetch(x, columns_y - 1)
+        send_y[0, 1, x] = fetch(x, 0)
+
+    peers = sum(jnp.where(present(axis, side), 1, 0) for axis, side in pairs)
+    pl.semaphore_wait(barrier, peers)
+    launch(0, 1)
+
+    @pl.loop(0, columns_x)
+    def _(x):
+        for y in range(1, columns_y - 1):
+            fetch(x, y)
+
+    for y in range(columns_y):
+        send_x[0, 0, y] = stretch[columns_x, y].astype(jnp.bfloat16)
+        send_x[0, 1, y] = stretch[1, y].astype(jnp.bfloat16)
+    launch(0, 0)
+
+    nothing = jnp.zeros((length, cases), jnp.float32)
+    for field in (stretch, dilation):
+        for y in range(columns_y):
+            field[0, y] = nothing
+            field[columns_x + 1, y] = nothing
+
+    columns = columns_x * columns_y
+    for first in range(0, 6 * columns, length):
+        turned = bond_live[first : first + length].astype(jnp.float32).T
+        for j in range(turned.shape[1]):
+            live[(first + j) // columns, (first + j) % columns] = jnp.broadcast_to(
+                turned[:, j : j + 1], (length, cases)
+            ).astype(jnp.bfloat16)
+
+    @pl.loop(0, columns_x)
+    def _(x):
+        for y in range(columns_y):
+            _, result, count = bond_sum(stretch, x, y)
+            other = displacement[x, y].astype(jnp.float32) + quarter * bricks[x, y].astype(
+                jnp.float32
+            )
+            dilation[x + 1, y] = (result - count * other) * (1.0 / 6.0)
+
+    def complete(axis, side):
+        def add(x, y, at):
+            bond = live[bonds[axis][side], x * columns_y + y].astype(jnp.float32)
+            value = recvs[axis][0, side, at].astype(jnp.float32)
+            dilation[x + 1, y] = dilation[x + 1, y] + bond * value * (1.0 / 6.0)
+
+        arrive(0, axis, side, add)
+
+    for axis, side in reversed(pairs):
+        complete(axis, side)
+
+    @pl.loop(0, columns_x)
+    def _(x):
+        send_y[1, 0, x] = dilation[x + 1, columns_y - 1].astype(jnp.bfloat16)
+        send_y[1, 1, x] = dilation[x + 1, 0].astype(jnp.bfloat16)
+
+    launch(1, 1)
+    for y in range(columns_y):
+        send_x[1, 0, y] = dilation[columns_x, y].astype(jnp.bfloat16)
+        send_x[1, 1, y] = dilation[1, y].astype(jnp.bfloat16)
+    launch(1, 0)
+
+    @pl.loop(0, columns_x)
+    def _(x):
+        for y in range(columns_y):
+            middle, result, count = bond_sum(dilation, x, y)
+            force = (6.0 * BOND_STIFFNESS) * middle + STATE_STIFFNESS * (result - count * middle)
+            value = displacement[x, y].astype(jnp.float32) + STEP_SIZE * force
+            stretch[x + 1, y] = value
+            if 0 < y < columns_y - 1:
+                moved[x, y] = value.astype(jnp.bfloat16)
+
+    def finish(axis, side):
+        def add(x, y, at):
+            bond = live[bonds[axis][side], x * columns_y + y].astype(jnp.float32)
+            value = recvs[axis][1, side, at].astype(jnp.float32)
+            value = stretch[x + 1, y] + (STEP_SIZE * STATE_STIFFNESS) * (bond * value)
+            stretch[x + 1, y] = value
+            if axis == 0 and 0 < y < columns_y - 1:
+                moved[x, y] = value.astype(jnp.bfloat16)
+
+        arrive(1, axis, side, add)
+
+    for axis, side in reversed(pairs):
+        finish(axis, side)
+
+    @pl.loop(0, columns_x)
+    def _(x):
+        for y in (0, columns_y - 1):
+            moved[x, y] = stretch[x + 1, y].astype(jnp.bfloat16)
+
+    for turn in (0, 1):
+        for axis, side in pairs:
+
+            @pl.when(present(axis, side))
+            def _():
+                edge_copy(turn, axis, side).wait_send()
+
+
+def mechanics(source_row, arrived, displacement, bond_live):
+    columns_x, columns_y, length, cases = displacement.shape
+    columns = columns_x * columns_y
+    vmem = pl.BlockSpec(memory_space=pltpu.VMEM)
+    field = pltpu.VMEM((columns_x + 2, columns_y, length, cases), jnp.float32)
+    edge_x = pltpu.VMEM((2, 2, columns_y, length, cases), jnp.bfloat16)
+    edge_y = pltpu.VMEM((2, 2, columns_x, length, cases), jnp.bfloat16)
+    out = jax.ShapeDtypeStruct(displacement.shape, jnp.bfloat16)
+    return pl.pallas_call(
+        mechanics_kernel,
+        out_shape=(out, out),
+        in_specs=[pl.BlockSpec(memory_space=pltpu.SMEM), vmem, vmem, vmem],
+        out_specs=(vmem, vmem),
+        scratch_shapes=[
+            field,
+            field,
+            pltpu.VMEM((6, columns, length, cases), jnp.bfloat16),
+            edge_x,
+            edge_y,
+            edge_x,
+            edge_y,
+            pltpu.SemaphoreType.DMA((2, 2, 2)),
+            pltpu.SemaphoreType.DMA((2, 2, 2)),
+        ],
+        compiler_params=pltpu.CompilerParams(
+            collective_id=1, has_side_effects=True, vmem_limit_bytes=50 * MIB
+        ),
+        name="mechanics",
+    )(source_row, arrived, displacement, bond_live.reshape(6 * columns, length))
 
 
 def local(
@@ -306,18 +503,7 @@
         conductance,
     )
     arrived = lax.all_to_all(outgoing, ("row", "col"), split_axis=0, concat_axis=0, tiled=True)
-    bricks = arrived[source_row].reshape(displacement.shape)
-
-    live = bond_live.astype(jnp.float32)[..., None]
-    count = jnp.sum(live, axis=0)
-    moving = displacement.astype(jnp.float32)
-    heat = (ALPHA_T * 0.5) * bricks.astype(jnp.float32)
-    dilatation = (bond_sum(moving - heat, live) - count * (moving + heat)) / 6.0
-    force = BOND_STIFFNESS * 6.0 * dilatation + STATE_STIFFNESS * (
-        bond_sum(dilatation, live) - count * dilatation
-    )
-    moved = (moving + STEP_SIZE * force).astype(jnp.bfloat16)
-    return (bricks, moved)
+    return mechanics(source_row, arrived, displacement, bond_live)
 
 
 def solution(mesh):

time: 280 us -> 253 us (0.904); the launches traced: 276 us -> 253 us
  waiting for transfers between devices: 77.9 us -> 0 us
  blocking collectives: 0 us -> 66.6 us
  Pallas kernels: 123 us -> 177 us
  starting transfers between devices: 41 us -> 0 us
  other arithmetic: 27.1 us -> 2.36 us
    all_to_all x0 -> x1, blocking collectives: none -> 66.6 us  [local(): lax.all_to_all(outgoing, ('row', 'col'), split_axis=0, concat_axis=0, til...]
    pallas_call x0 -> x1, Pallas kernels: none -> 53.9 us  [mechanics(): pl.pallas_call(mechanics_kernel, out_shape=(out, out), in_specs=[pl.Block...]
    all_to_all x1 -> x0, waiting for transfers between devices: 46.9 us -> none  [local(): lax.all_to_all(outgoing, ('row', 'col'), split_axis=0, concat_axis=0, til...]
    ppermute x8 -> x0, waiting for transfers between devices: 30.9 us -> none  [edges(): return (lax.ppermute(last, axis, up), lax.ppermute(leading, axis, down))]
    convert_element_type x12 -> x0, other arithmetic: 23.9 us -> none  [the longest x2 12.8 us: bond_sum(): sent = field.astype(jnp.bfloat16)]
    ppermute x8 -> x0, starting transfers between devices: 22.9 us -> none  [edges(): return (lax.ppermute(last, axis, up), lax.ppermute(leading, axis, down))]
    all_to_all x1 -> x0, starting transfers between devices: 18.1 us -> none  [local(): lax.all_to_all(outgoing, ('row', 'col'), split_axis=0, concat_axis=0, til...]
    unnamed x9, local copies, waits for them, and re-layouts: 1.51 us -> 4.45 us
  transfers between devices with their start and end apart: 9 -> 0, of which waited for: 5 -> 0; matrix products, arithmetic and copies ran while one was open for 0% -> 0% of each run, Pallas kernels for 0% -> 0%
where the time goes in v2:
time: 253 us
  Pallas kernels  177 us (70%)
  blocking collectives  66.6 us (26%)
  local copies, waits for them, and re-layouts  6.52 us (3%)
    pallas_call x1, Pallas kernels, chebyshev(): pl.pallas_call(chebyshev_kernel, out_shape=jax.ShapeDtypeStruct((route.sh...  123 us
    all_to_all x1, blocking collectives, local(): lax.all_to_all(outgoing, ('row', 'col'), split_axis=0, concat_axis=0, til...  66.6 us
    pallas_call x1, Pallas kernels, mechanics(): pl.pallas_call(mechanics_kernel, out_shape=(out, out), in_specs=[pl.Block...  53.9 us

profile of v2, /device:TPU:8, one launch (start us, length us, event | category | flops | bytes accessed | tf_op | source)
XLA Modules:
  0.0 252.7 jit_solution(15999193511903585546)
XLA Ops:
  0.6 0.0 copy-start
  0.7 1.3 reshape.44.send_list
  1.9 0.0 copy-done
  1.9 0.1 constant_dynamic-slice_fusion
  2.0 0.1 select_reduce_fusion.1
  2.1 0.2 convert_reduce_fusion
  2.3 1.4 convert_bitcast_fusion.active
  3.7 0.8 copy.12
  4.5 0.7 reshape.43.pattern
  5.2 0.7 select_reduce_fusion.route
  5.9 122.7 %chebyshev.1 = bf16[64,128,128]{2,1,0:T(8,128)(2,1)} custom-call(s32[448]{0:T(512)} %reshape.43.pattern, s32[64]{0:T(128)} %reshape.44.send_list, s32[64]{0:T(128)} %select_reduce_fusion.route, bf16[64,128,128]{2,1,0:T(8,128)(2,1)} %bitcast.10, f32[64,128]{1,0:T(8,128)} %convert_bitcast_fusion.active, f32[64,128]{1,0:T(8,128)} %bitcast.11, ...), custom_call_target="tpu_custom_call" | custom-call | tf_op jit(solution)/shard_map/chebyshev/pallas_call | solution.py:209
  128.6 0.0 copy-start.1
  128.6 66.6 %all_to_all.5.arrived = bf16[64,128,128]{2,1,0:T(8,128)(2,1)} all-to-all(bf16[64,128,128]{2,1,0:T(8,128)(2,1)} %chebyshev.1), channel_id=1, replica_groups=mesh['row'=4,'col'=8] {'row','col'}, dimensions={0} | all-to-all | bytes 4194304 | tf_op jit(solution)/shard_map/all_to_all | solution.py:505
  195.1 0.0 copy-done.1
  195.1 53.9 %mechanics.1 = (bf16[16,4,128,128]{3,2,1,0:T(8,128)(2,1)S(1)}, bf16[16,4,128,128]{3,2,1,0:T(8,128)(2,1)}) custom-call(s32[64]{0:T(128)S(1)} %get-tuple-element.5.source_row, bf16[64,128,128]{2,1,0:T(8,128)(2,1)} %all_to_all.5.arrived, bf16[16,4,128,128]{3,2,1,0:T(8,128)(2,1)} %displacement.1, s32[384,128]{1,0:T(8,128)S(1)} %bitcast.9), custom_call_target="tpu_custom_call" | custom-call | tf_op jit(solution)/shard_map/mechanics/pallas_call | solution.py:439
  249.0 0.0 copy-start.2
  249.0 1.3 copy.15
  250.4 1.0 copy-done.2
  251.4 1.3 copy.16
  (2 shorter events, 0.0 us)
Async XLA Ops:
  0.6 1.3 copy-start
  128.6 66.6 %copy-start.1 = (s32[6,16,4,128]{3,2,1,0:T(4,128)S(1)}, s32[6,16,4,128]{3,2,1,0:T(4,128)}, u32[]{:S(2)}) copy-start(s32[6,16,4,128]{3,2,1,0:T(4,128)} %param.17) | copy-start | bytes 589828
  249.0 2.3 copy-start.2

commit v3 on v2

--- a/solution.py
+++ b/solution.py
@@ -54,6 +54,10 @@
     tile_sem,
     send_sem,
     recv_sem,
+    brick_send_sem,
+    brick_recv_sem,
+    kept_sem,
+    stage,
 ):
     rows, cols = lax.axis_size("row"), lax.axis_size("col")
     devices = rows * cols
@@ -74,11 +78,12 @@
         return (lax.div(index, cols), lax.rem(index, cols))
 
     barrier = pltpu.get_barrier_semaphore()
-    for step in GHOST_STEPS:
-
-        @pl.when(inside(me + step))
-        def _():
-            pl.semaphore_signal(barrier, inc=1, device_id=place(me + step), device_id_type=MESH)
+
+    @pl.loop(1, devices)
+    def _(k):
+        pl.semaphore_signal(
+            barrier, inc=1, device_id=place(lax.rem(me + k, devices)), device_id_type=MESH
+        )
 
     def ghost_copy(it, group):
         return pltpu.make_async_remote_copy(
@@ -90,7 +95,7 @@
             device_id_type=MESH,
         )
 
-    wide = jnp.concatenate([active[...], diagonal[...]], axis=0).T
+    wide = jnp.concatenate([active[...].astype(jnp.float32), diagonal[...]], axis=0).T
     for b in range(blocks):
         column = jnp.broadcast_to(wide[:, b : b + 1], (length, cases))
         active_wide[b] = column.astype(jnp.bfloat16)
@@ -105,8 +110,7 @@
         masked[b] = value
         ext0[b] = value
 
-    peers = sum(jnp.where(inside(me + step), 1, 0) for step in GHOST_STEPS)
-    pl.semaphore_wait(barrier, peers)
+    pl.semaphore_wait(barrier, devices - 1)
 
     for it in range(ITERS):
         ext = exts[it]
@@ -120,7 +124,7 @@
 
             @pl.loop(0, cap)
             def _(j):
-                outgoing[group * cap + j] = masked[send_list[group * cap + j]]
+                outgoing[group * cap + j] = masked[send_list[0, group, j]]
 
             @pl.when(inside(me + step))
             def _():
@@ -160,7 +164,7 @@
                 ghost_copy(it, group).wait_recv()
 
         old_weight, res_weight = weights[it]
-        unroll = 2
+        unroll = 4
 
         @pl.loop(0, blocks // unroll)
         def _(pair):
@@ -168,7 +172,7 @@
                 b = pair * unroll + part
                 chosen = [ext[blocks + b]]
                 for k in range(2, tile_count):
-                    chosen.append(ext[pattern[b * tile_count + k]])
+                    chosen.append(ext[pattern[b, k]])
                 row = jnp.concatenate([tiles[b, k] for k in range(1, tile_count)], axis=1)
                 far = jnp.dot(
                     row, jnp.concatenate(chosen, axis=0), preferred_element_type=jnp.float32
@@ -185,9 +189,43 @@
                 else:
                     masked[b] = (total[b] + held).astype(jnp.bfloat16)
 
-    @pl.loop(0, out.shape[0])
-    def _(j):
-        out[j] = masked[route[j]]
+    each = stage.shape[0] // devices
+
+    def pick(index):
+        for j in range(each):
+            stage[index * each + j] = masked[route[index * each + j]]
+
+    def brick_copy(source, owner, index):
+        return pltpu.make_async_remote_copy(
+            src_ref=stage.at[pl.ds(source * each, each)],
+            dst_ref=out.at[pl.ds(owner * each, each)],
+            send_sem=brick_send_sem.at[source],
+            recv_sem=brick_recv_sem.at[owner],
+            device_id=place(index),
+            device_id_type=MESH,
+        )
+
+    @pl.loop(1, devices)
+    def _(k):
+        index = lax.rem(me + k, devices)
+        pick(index)
+        brick_copy(index, me, index).start()
+
+    pick(me)
+    own_rows = pl.ds(me * each, each)
+    kept = pltpu.make_async_copy(stage.at[own_rows], out.at[own_rows], kept_sem)
+    kept.start()
+    kept.wait()
+
+    @pl.loop(1, devices)
+    def _(k):
+        index = lax.rem(me + k, devices)
+        brick_copy(index, me, index).wait_send()
+
+    @pl.loop(1, devices)
+    def _(k):
+        index = lax.rem(me + devices - k, devices)
+        brick_copy(index, index, index).wait_recv()
 
     for group, step in enumerate(GHOST_STEPS):
 
@@ -199,7 +237,8 @@
 def chebyshev(pattern, send_list, route, heat, active, diagonal, conductance):
     blocks, length, cases = heat.shape
     tile_count = conductance.shape[1]
-    ghosts = send_list.shape[0]
+    ghosts = send_list.shape[1] * send_list.shape[2]
+    devices = lax.axis_size(("row", "col"))
     smem = pl.BlockSpec(memory_space=pltpu.SMEM)
     vmem = pl.BlockSpec(memory_space=pltpu.VMEM)
     hbm = pl.BlockSpec(memory_space=pl.ANY)
@@ -210,7 +249,7 @@
         chebyshev_kernel,
         out_shape=jax.ShapeDtypeStruct((route.shape[0], length, cases), jnp.bfloat16),
         in_specs=[smem, smem, smem, vmem, vmem, vmem, hbm],
-        out_specs=vmem,
+        out_specs=hbm,
         scratch_shapes=[
             pltpu.VMEM(conductance.shape, jnp.bfloat16),
             ext,
@@ -226,6 +265,10 @@
             pltpu.SemaphoreType.DMA,
             pltpu.SemaphoreType.DMA((ITERS, len(GHOST_STEPS))),
             pltpu.SemaphoreType.DMA((ITERS, len(GHOST_STEPS))),
+            pltpu.SemaphoreType.DMA((devices,)),
+            pltpu.SemaphoreType.DMA((devices,)),
+            pltpu.SemaphoreType.DMA,
+            pltpu.VMEM((route.shape[0], length, cases), jnp.bfloat16),
         ],
         compiler_params=pltpu.CompilerParams(
             collective_id=0, has_side_effects=True, vmem_limit_bytes=58 * MIB
@@ -493,16 +536,15 @@
     route = jnp.sum(jnp.where(target[None, :] == places[:, None], block_of[None, :], 0), axis=1)
     source_row = ((me - distance + devices) % devices) * cap + rank
 
-    outgoing = chebyshev(
-        pattern.reshape(-1),
-        send_list.reshape(-1),
+    arrived = chebyshev(
+        pattern,
+        send_list,
         route,
         heat_source.reshape(blocks, length, cases),
-        active.astype(jnp.float32).reshape(blocks, length),
+        active.reshape(blocks, length),
         diagonal.reshape(blocks, length),
         conductance,
     )
-    arrived = lax.all_to_all(outgoing, ("row", "col"), split_axis=0, concat_axis=0, tiled=True)
     return mechanics(source_row, arrived, displacement, bond_live)
 
 

time: 253 us -> 239 us (0.945); the launches traced: 253 us -> 234 us
  blocking collectives: 66.6 us -> 0 us
  Pallas kernels: 177 us -> 226 us
    all_to_all x1 -> x0, blocking collectives: 66.6 us -> none  [local(): lax.all_to_all(outgoing, ('row', 'col'), split_axis=0, concat_axis=0, til...]
    pallas_call x1, Pallas kernels: 123 us -> 166 us  [chebyshev(): pl.pallas_call(chebyshev_kernel, out_shape=jax.ShapeDtypeStruct((route.sh...]
    pallas_call x1, Pallas kernels: 53.9 us -> 60 us  [mechanics(): pl.pallas_call(mechanics_kernel, out_shape=(out, out), in_specs=[pl.Block...]
where the time goes in v3:
time: 239 us; the launch traced here: 234 us
  Pallas kernels  226 us (95%)
  local copies, waits for them, and re-layouts  5.83 us (2%)
    pallas_call x1, Pallas kernels, chebyshev(): pl.pallas_call(chebyshev_kernel, out_shape=jax.ShapeDtypeStruct((route.sh...  166 us
    pallas_call x1, Pallas kernels, mechanics(): pl.pallas_call(mechanics_kernel, out_shape=(out, out), in_specs=[pl.Block...  60 us
    unnamed x9, local copies, waits for them, and re-layouts  5.76 us

profile of v3, /device:TPU:8, one launch (start us, length us, event | category | flops | bytes accessed | tf_op | source)
XLA Modules:
  0.0 233.9 jit_solution(15321044938808359986)
XLA Ops:
  0.6 0.0 copy-start
  0.7 0.7 copy-done
  1.4 0.1 constant_dynamic-slice_fusion
  1.4 0.1 select_reduce_fusion.1
  1.6 0.2 convert_reduce_fusion
  1.8 0.6 select_reduce_fusion.route
  2.4 1.4 copy.12.pattern
  3.8 0.0 copy-start.1
  3.8 166.4 %chebyshev.1.arrived = bf16[64,128,128]{2,1,0:T(8,128)(2,1)} custom-call(s32[64,7]{1,0:T(8,128)} %copy.12.pattern, s32[1,4,16]{2,1,0:T(4,128)} %send_list.1, s32[64]{0:T(128)} %select_reduce_fusion.route, bf16[64,128,128]{2,1,0:T(8,128)(2,1)} %bitcast.9, s32[64,128]{1,0:T(8,128)} %bitcast.10, f32[64,128]{1,0:T(8,128)} %bitcast.11, ...), custom_call_target="tpu_custom_call" | custom-call | tf_op jit(solution)/shard_map/chebyshev/pallas_call | solution.py:248
  170.2 0.0 copy-done.1
  170.2 60.0 %mechanics.1 = (bf16[16,4,128,128]{3,2,1,0:T(8,128)(2,1)S(1)}, bf16[16,4,128,128]{3,2,1,0:T(8,128)(2,1)}) custom-call(s32[64]{0:T(128)S(1)} %get-tuple-element.5.source_row, bf16[64,128,128]{2,1,0:T(8,128)(2,1)} %chebyshev.1.arrived, bf16[16,4,128,128]{3,2,1,0:T(8,128)(2,1)} %displacement.1, s32[384,128]{1,0:T(8,128)S(1)} %bitcast.8), custom_call_target="tpu_custom_call" | custom-call | tf_op jit(solution)/shard_map/mechanics/pallas_call | solution.py:482
  230.2 0.0 copy-start.2
  230.2 1.3 copy.15
  231.6 1.0 copy-done.2
  232.6 1.3 copy.16
  (2 shorter events, 0.0 us)
Async XLA Ops:
  0.6 0.7 copy-start
  3.8 166.4 %copy-start.1 = (s32[6,16,4,128]{3,2,1,0:T(4,128)S(1)}, s32[6,16,4,128]{3,2,1,0:T(4,128)}, u32[]{:S(2)}) copy-start(s32[6,16,4,128]{3,2,1,0:T(4,128)} %param.17) | copy-start | bytes 589828
  230.2 2.3 %copy-start.2 = (bf16[16,4,128,128]{3,2,1,0:T(8,128)(2,1)S(1)}, bf16[16,4,128,128]{3,2,1,0:T(8,128)(2,1)}, u32[]{:S(2)}) copy-start(bf16[16,4,128,128]{3,2,1,0:T(8,128)(2,1)} %get-tuple-element.11) | copy-start | bytes 6291460
